TPU v7x, 32 devices: a whole 2x2x4 slice. The times are simulated.
32 devices in a mesh: gx: 4 (over y, x), gy: 8 (over z, core).
Axes of the slice: x: 2, y: 2, z: 4, core: 2. Of those that a mesh axis runs over, the one named last changes fastest.
Arguments:
- density_one: float32 [512, 512, 512], P('gx', 'gy'), may hold values from -6 to 6
- density_two: float32 [512, 512, 512], P('gx', 'gy'), may hold values from -6 to 6
Outputs:
- correlation: float32 [512, 512, 512], P('gx', 'gy')
All inputs are finite; a program needn't handle non-finite values.
Results may differ from a plain program's by a relative error of at most 0.00013.
Values sent between devices are 32-bit elements; how exact they have to be, the bound alone decides.
A program may use at most 256 MiB of HBM per device.

v0:
```python
import math

import jax
import jax.numpy as jnp
from jax import lax
from jax.sharding import PartitionSpec as P

exact_mode = lax.Precision.HIGHEST


def phases(numerator, denominator):
    radians = (numerator % denominator).astype(jnp.float32) * (2.0 * math.pi / denominator)
    return (jnp.cos(radians), jnp.sin(radians))


def complex_table(length, direction):
    positions = jnp.arange(length, dtype=jnp.int32)
    cosines, sines_raw = phases(positions[:, None] * positions[None, :], length)
    signed = direction * sines_raw
    real_rows = jnp.stack([cosines, signed], axis=1)
    imag_rows = jnp.stack([-signed, cosines], axis=1)
    return jnp.stack([real_rows, imag_rows], axis=0)


def depth_tables(depth_cells, count_x, count_y):
    half_depth = depth_cells // 2
    kz_slices = half_depth // (count_x * count_y)
    row_ids = jnp.arange(2 * half_depth, dtype=jnp.int32)
    within = row_ids % kz_slices
    imag_flag = row_ids // kz_slices % 2
    row_block = row_ids // (2 * kz_slices)
    row_block = row_block % count_y * count_x + row_block // count_y
    wave_number = row_block * kz_slices + within
    cell_ids = jnp.arange(depth_cells, dtype=jnp.int32)
    cosines, sines_raw = phases(wave_number[:, None] * cell_ids[None, :], depth_cells)
    is_imag = (imag_flag == 1)[:, None]
    forward = jnp.where(is_imag, -sines_raw, cosines)
    weight = jnp.where(wave_number == 0, 1.0, 2.0)[:, None]
    inverse = jnp.where(is_imag, -weight * sines_raw, weight * cosines)
    return (forward, inverse)


def on_device(density_one, density_two):
    count_x = lax.axis_size("gx")
    count_y = lax.axis_size("gy")
    x_local, y_local, depth_cells = density_one.shape
    grid_x = x_local * count_x
    grid_y = y_local * count_y
    kz_slices = depth_cells // 2 // (count_x * count_y)
    columns = x_local * y_local
    cell_total = float(grid_x * grid_y * depth_cells)
    forward_depth, inverse_depth = depth_tables(depth_cells, count_x, count_y)

    def depth_forward(density):
        flat_lines = density.reshape(columns, depth_cells)
        return lax.dot_general(
            forward_depth, flat_lines, (((1,), (1,)), ((), ())), precision=exact_mode
        )

    spectra = jnp.stack([depth_forward(density_one), depth_forward(density_two)])
    y_forward = complex_table(grid_y, -1.0).reshape(2, count_y, y_local, 2, grid_y)
    y_inverse = complex_table(grid_y, 1.0).reshape(2, grid_y, 2, count_y, y_local)
    block_forward = complex_table(count_x, -1.0)
    block_inverse = complex_table(count_x, 1.0)
    local_forward = complex_table(x_local, -1.0)
    sent = spectra.reshape(2, count_x * count_y, 2 * kz_slices, columns)
    moved = lax.all_to_all(sent, ("gx", "gy"), split_axis=1, concat_axis=1, tiled=True)
    moved = moved.reshape(2, count_x, count_y, 2, kz_slices, x_local, y_local)
    planes = jnp.einsum("fdspkjy,psyrq->fdrkjq", moved, y_forward, precision=exact_mode)
    aligned = jnp.einsum("fdpkjq,pdra->farkjq", planes, block_forward, precision=exact_mode)
    twiddle_cos, twiddle_sin = phases(
        jnp.arange(count_x, dtype=jnp.int32)[:, None]
        * jnp.arange(x_local, dtype=jnp.int32)[None, :],
        grid_x,
    )
    forward_cos = twiddle_cos[None, :, None, :, None]
    forward_sin = twiddle_sin[None, :, None, :, None]
    real_part = aligned[:, :, 0]
    imag_part = aligned[:, :, 1]
    turned = jnp.stack(
        [
            real_part * forward_cos + imag_part * forward_sin,
            imag_part * forward_cos - real_part * forward_sin,
        ],
        axis=2,
    )
    spectra_k = jnp.einsum("fapkjq,pjrb->farkbq", turned, local_forward, precision=exact_mode)
    power = (
        spectra_k[0, :, 0] * spectra_k[1, :, 0] + spectra_k[0, :, 1] * spectra_k[1, :, 1]
    ) / cell_total
    wave_x = (
        jnp.arange(count_x, dtype=jnp.int32)[:, None]
        + count_x * jnp.arange(x_local, dtype=jnp.int32)[None, :]
    )
    keep_x = (wave_x != grid_x // 2)[:, None, :, None]
    keep_y = (jnp.arange(grid_y, dtype=jnp.int32) != grid_y // 2)[None, None, None, :]
    power = jnp.where(keep_x & keep_y, power, 0.0)
    cos_local, sin_local = phases(
        jnp.arange(x_local, dtype=jnp.int32)[:, None]
        * jnp.arange(x_local, dtype=jnp.int32)[None, :],
        x_local,
    )
    real_table = jnp.stack([cos_local, sin_local], axis=1)
    lines = jnp.einsum("akbq,brj->arkjq", power, real_table, precision=exact_mode)
    inverse_cos = twiddle_cos[:, None, :, None]
    inverse_sin = twiddle_sin[:, None, :, None]
    real_part = lines[:, 0]
    imag_part = lines[:, 1]
    unturned = jnp.stack(
        [
            real_part * inverse_cos - imag_part * inverse_sin,
            imag_part * inverse_cos + real_part * inverse_sin,
        ],
        axis=1,
    )[None]
    blocks = jnp.einsum("fapkjq,pard->fdrkjq", unturned, block_inverse, precision=exact_mode)
    back_lines = jnp.einsum("fdpkjq,pqrsy->fdsrkjy", blocks, y_inverse, precision=exact_mode)
    sent_back = back_lines.reshape(1, count_x * count_y, 2 * kz_slices, columns)
    rows_back = lax.all_to_all(sent_back, ("gx", "gy"), split_axis=1, concat_axis=1, tiled=True)
    rows_flat = rows_back.reshape(2 * kz_slices * count_x * count_y, columns)
    correlation = lax.dot_general(
        rows_flat, inverse_depth, (((0,), (0,)), ((), ())), precision=exact_mode
    )
    correlation = correlation * (1.0 / math.sqrt(cell_total))
    return correlation.reshape(x_local, y_local, depth_cells)


def solution(mesh):
    return jax.shard_map(
        on_device,
        mesh=mesh,
        in_specs=(P("gx", "gy", None), P("gx", "gy", None)),
        out_specs=P("gx", "gy", None),
        check_vma=False,
    )
```

profile of v0, /device:TPU:0, one launch (start us, length us, event | category | flops | bytes accessed | tf_op | source)
XLA Modules:
  0.0 2118.7 jit_solution(7374333647486353023)
XLA Ops:
  0.1 0.0 slice-start
  0.1 4.3 fusion.212
  4.4 4.3 fusion.214
  8.7 0.0 slice-start.1
  8.7 0.0 slice-start.2
  8.7 0.0 slice-start.3
  8.7 32.4 %convolution_bitcast_fusion = f32[1,32,16,8192]{3,2,1,0:T(8,128)} fusion(f32[8192,512,1]{1,0,2:T(8,128)} %bitcast.172, f32[32,16,512]{2,1,0:T(8,128)S(1)} %fusion.212), kind=kOutput, calls=%fused_computation.18 | convolution fusion | flops 25769803776 | bytes 34603008 | tf_op jit(solution)/shard_map/dot_general | solution.py:56
  41.1 0.0 slice-done
  41.1 0.0 slice-done.1
  41.1 0.0 slice-done.2
  41.1 0.0 slice-done.3
  41.2 29.7 %convolution_bitcast_fusion.1 = f32[1,32,16,8192]{3,2,1,0:T(8,128)} fusion(f32[8192,512,1]{1,0,2:T(8,128)S(1)} %bitcast.175, f32[32,16,512]{2,1,0:T(8,128)S(1)} %fusion.214), kind=kOutput, calls=%fused_computation.19 | convolution fusion | flops 25769803776 | bytes 34603008 | tf_op jit(solution)/shard_map/dot_general | solution.py:56
  70.8 12.4 pad_maximum_fusion
  83.3 11.1 copy.45
  94.3 7.7 all-to-all-start
  102.0 0.1 fusion.171
  102.1 0.1 fusion.168
  102.1 0.1 broadcast_multiply_fusion.1
  102.2 0.1 copy.44
  102.3 0.1 copy.43
  102.4 0.1 fusion.165
  102.5 0.0 copy-start.11
  102.5 0.1 copy.50
  102.6 0.4 copy-done.9
  103.0 0.1 copy.49
  103.1 0.7 copy.41
  103.8 0.7 copy.40
  104.5 0.0 copy-done.11
  104.5 0.3 fusion.115
  104.8 0.9 fusion.113
  105.7 0.3 broadcast_multiply_fusion
  106.0 0.0 copy-start.4
  106.0 0.6 copy-done.4
  106.6 0.7 fusion.105
  107.3 4.2 sine_multiply_fusion
  111.5 2.6 maximum_bitcast_fusion.21
  114.1 0.9 broadcast_and_fusion
  115.0 6.0 fusion.96
  121.0 705.1 %all-to-all-done = f32[2,32,16,8192]{3,2,0,1:T(8,128)} async-done(((f32[2,32,16,8192]{3,2,0,1:T(8,128)}), f32[2,32,16,8192]{3,2,0,1:T(8,128)}, u32[]{:S(2)}, u32[]{:S(2)}) %all-to-all-start) | async-done | bytes 33554464 | tf_op jit(solution)/shard_map/all_to_all | solution.py:67
  826.1 52.6 %reshape.673 = f32[2,4,8,2,8,128,64]{6,5,4,3,0,2,1:T(8,128)} reshape(f32[2,32,16,8192]{3,2,0,1:T(8,128)} %all-to-all-done) | data formatting | bytes 67108864 | tf_op jit(solution)/shard_map/reshape | solution.py:68
  878.7 433.2 %fusion.18 = f32[2,4,2,8,128,512]{4,5,3,1,0,2:T(8,128)} fusion(f32[2,4,8,2,8,128,64]{6,5,4,3,0,2,1:T(8,128)} %reshape.673, f32[2,8,64,2,512,1,1,1]{4,2,1,0,7,6,5,3:T(8,128)} %maximum_bitcast_fusion.21), kind=kOutput, calls=%fused_computation.21 | convolution fusion | flops 103079215104 | bytes 71303168 | tf_op jit(solution)/shard_map/fdspkjy,psyrq->fdrkjq/dot_general | solution.py:69
  1311.9 39.3 %copy.48 = f32[2,4,2,8,128,512]{5,1,2,4,3,0:T(4,128)} copy(f32[2,4,2,8,128,512]{4,5,3,1,0,2:T(8,128)} %fusion.18) | data formatting | bytes 67108864 | tf_op jit(solution)/shard_map/fdspkjy,psyrq->fdrkjq/transpose | solution.py:69
  1351.1 74.9 %fusion.7 = f32[2,4,2,8,128,512]{5,1,4,3,0,2:T(4,128)} fusion(f32[2,4,2,8,128,512]{5,1,2,4,3,0:T(4,128)} %copy.48, f32[2,4,2,4,1,1,1]{1,3,0,6,5,4,2:T(4,128)S(1)} %maximum_bitcast_fusion.20), kind=kOutput, calls=%fused_computation.9 | convolution fusion | flops 805306368 | bytes 67109120 | tf_op jit(solution)/shard_map/fdpkjq,pdra->farkjq/dot_general | solution.py:70
  1426.0 27.3 %multiply_add_fusion = (f32[2,4,1,8,128,512]{5,1,4,3,0,2:T(4,128)}, f32[2,4,1,8,128,512]{5,1,4,3,0,2:T(4,128)}) fusion(f32[2,4,2,8,128,512]{5,1,4,3,0,2:T(4,128)} %fusion.7, f32[4,128]{0,1:T(8,128)S(1)} %copy.50, f32[4,128]{0,1:T(8,128)S(1)} %copy.49), kind=kLoop, calls=%fused_computation.17 | loop fusion | flops 25165824 | bytes 67112960 | tf_op jit(solution)/shard_map/add | solution.py:82
  1453.3 23.0 %pad_maximum_fusion.1 = f32[2,4,2,8,128,512]{5,1,4,3,0,2:T(4,128)} fusion(f32[2,4,1,8,128,512]{5,1,4,3,0,2:T(4,128)} %get-tuple-element.6, f32[2,4,1,8,128,512]{5,1,4,3,0,2:T(4,128)} %get-tuple-element.5), kind=kLoop, calls=%fused_computation.3 | loop fusion | flops 8388608 | bytes 67108864 | tf_op jit(solution)/shard_map/stack | solution.py:80
  1476.3 0.0 copy-done.6
  1476.3 0.0 copy-done.7
  1476.3 0.0 copy-start
  1476.3 0.0 copy-start.5
  1476.3 45.4 %fusion.15 = f32[2,4,2,8,128,512]{5,4,3,1,0,2:T(8,128)} fusion(f32[2,4,2,8,128,512]{5,1,4,3,0,2:T(4,128)} %pad_maximum_fusion.1, f32[1,128,2,128]{1,3,0,2:T(8,128)S(1)} %copy-done.7, f32[1,128,2,128]{1,3,0,2:T(8,128)S(1)} %copy-done.6), kind=kOutput, calls=%fused_computation.20 | convolution fusion | flops 25769869312 | bytes 67371008 | tf_op jit(solution)/shard_map/fapkjq,pjrb->farkbq/dot_general | solution.py:87
  1521.8 0.0 copy-done.5
  1521.8 23.0 %fusion.33 = f32[4,2,8,128,512]{4,3,2,0,1:T(8,128)} fusion(f32[2,4,2,8,128,512]{5,4,3,1,0,2:T(8,128)} %fusion.15, pred[4,128,512]{2,1,0:T(8,128)(4,1)S(1)} %copy-done, f32[128,1,128]{0,2,1:T(8,128)S(1)} %copy-done.5, f32[128,1,128]{0,2,1:T(8,128)S(1)} %copy-done.8), kind=kOutput, calls=%fused_computation.36 | convolution fusion | flops 6452969472 | bytes 50724864 | tf_op jit(solution)/shard_map/akbq,brj->arkjq/dot_general | solution.py:104
  1544.8 0.0 copy-done.12
  1544.8 11.0 multiply_subtract_fusion.1
  1555.8 6.9 pad_maximum_fusion.2
  1562.8 44.0 %fusion.21 = f32[4,2,8,128,512,1,1]{4,0,3,2,1,6,5:T(4,128)} fusion(f32[4,2,8,128,512]{4,3,2,0,1:T(8,128)S(1)} %pad_maximum_fusion.2, f32[1,4,2,4]{1,3,0,2:T(4,128)S(1)} %copy-done.13, f32[1,4,2,4]{1,3,0,2:T(4,128)S(1)} %copy-done.14), kind=kOutput, calls=%fused_computation.23 | convolution fusion | flops 402653248 | bytes 33554688 | tf_op jit(solution)/shard_map/fapkjq,pard->fdrkjq/dot_general | solution.py:116
  1606.8 0.0 copy-done.2
  1606.8 60.9 %fusion.36 = f32[1,4,8,2,8,128,64]{5,6,4,1,2,3,0:T(8,128)} fusion(f32[4,2,8,128,512,1,1]{4,0,3,2,1,6,5:T(4,128)} %fusion.21, f32[1,512,1,8,64]{1,4,0,3,2:T(8,128)S(1)} %copy-done.3, f32[1,512,1,8,64]{1,4,0,3,2:T(8,128)S(1)} %copy-done.2, f32[1,512,1,8,64]{1,4,0,3,2:T(8,128)S(1)} %copy-done.1), kind=kOutput, calls=%fused_computation.37 | convolution fusion | flops 51542753280 | bytes 36700160 | tf_op jit(solution)/shard_map/fdpkjq,pqrsy->fdsrkjy/dot_general | solution.py:117
  1667.7 23.0 %copy.54 = f32[1,4,8,2,8,128,64]{6,5,4,3,2,1,0:T(8,128)} copy(f32[1,4,8,2,8,128,64]{5,6,4,1,2,3,0:T(8,128)} %fusion.36) | data formatting | bytes 33554432 | tf_op jit(solution)/shard_map/fdpkjq,pqrsy->fdsrkjy/transpose | solution.py:117
  1690.8 27.9 %reshape.651 = f32[1,32,16,8192]{3,2,1,0:T(8,128)} reshape(f32[1,4,8,2,8,128,64]{6,5,4,3,2,1,0:T(8,128)} %copy.54) | data formatting | bytes 33554432 | tf_op jit(solution)/shard_map/reshape | solution.py:118
  1718.7 3.9 all-to-all-start.1
  1722.6 4.4 fusion.217
  1727.0 360.1 %all-to-all-done.1 = f32[1,32,16,8192]{3,2,0,1:T(8,128)} async-done(((f32[1,32,16,8192]{3,2,0,1:T(8,128)}), f32[1,32,16,8192]{3,2,0,1:T(8,128)}, u32[]{:S(2)}, u32[]{:S(2)}) %all-to-all-start.1) | async-done | bytes 16777248 | tf_op jit(solution)/shard_map/all_to_all | solution.py:119
  2087.1 31.2 %convolution_multiply_fusion = f32[8192,512]{1,0:T(8,128)} fusion(f32[512,8192]{1,0:T(8,128)} %bitcast.55, f32[512,512]{1,0:T(8,128)S(1)} %fusion.217), kind=kOutput, calls=%fused_computation.22 | convolution fusion | flops 25773998080 | bytes 34603008 | tf_op jit(solution)/shard_map/dot_general | solution.py:121
  (30 shorter events, 0.2 us)
Async XLA Ops:
  0.1 41.1 %slice-start = ((s8[16777216]{0:T(1024)(128)(4,1)}), s8[4194304]{0:T(1024)(128)(4,1)S(1)}, s32[]{:S(2)}) async-start(s8[16777216]{0:T(1024)(128)(4,1)} %bitcast.173), calls=%async_computation.2 | async-start | bytes 8388608
  8.7 32.5 %slice-start.1 = ((s8[16777216]{0:T(1024)(128)(4,1)}), s8[4194304]{0:T(1024)(128)(4,1)S(1)}, s32[]{:S(2)}) async-start(s8[16777216]{0:T(1024)(128)(4,1)} %bitcast.173), calls=%async_computation.3 | async-start | bytes 8388608
  8.7 32.4 %slice-start.2 = ((s8[16777216]{0:T(1024)(128)(4,1)}), s8[4194304]{0:T(1024)(128)(4,1)S(1)}, s32[]{:S(2)}) async-start(s8[16777216]{0:T(1024)(128)(4,1)} %bitcast.173), calls=%async_computation.4 | async-start | bytes 8388608
  8.7 32.4 %slice-start.3 = ((s8[16777216]{0:T(1024)(128)(4,1)}), s8[4194304]{0:T(1024)(128)(4,1)S(1)}, s32[]{:S(2)}) async-start(s8[16777216]{0:T(1024)(128)(4,1)} %bitcast.173), calls=%async_computation.5 | async-start | bytes 8388608
  94.3 731.7 %all-to-all-start = ((f32[2,32,16,8192]{3,2,0,1:T(8,128)}), f32[2,32,16,8192]{3,2,0,1:T(8,128)}, u32[]{:S(2)}, u32[]{:S(2)}) async-start(f32[2,32,16,8192]{3,2,0,1:T(8,128)} %copy.45), calls=%async_computation | async-start | bytes 67108864 | tf_op jit(solution)/shard_map/all_to_all | solution.py:67
  102.5 0.5 copy-start.9
  102.5 2.0 copy-start.11
  106.0 0.6 copy-start.4
  1453.3 23.0 %copy-start.6 = (f32[1,128,2,128]{1,3,0,2:T(8,128)S(1)}, f32[1,128,2,128]{1,3,0,2:T(8,128)}, u32[]{:S(2)}) copy-start(f32[1,128,2,128]{1,3,0,2:T(8,128)} %get-tuple-element.9) | copy-start | bytes 393220
  1453.3 23.0 %copy-start.7 = (f32[1,128,2,128]{1,3,0,2:T(8,128)S(1)}, f32[1,128,2,128]{1,3,0,2:T(8,128)}, u32[]{:S(2)}) copy-start(f32[1,128,2,128]{1,3,0,2:T(8,128)} %get-tuple-element.10) | copy-start | bytes 393220
  1476.3 45.5 %copy-start = (pred[4,128,512]{2,1,0:T(8,128)(4,1)S(1)}, pred[4,128,512]{2,1,0:T(8,128)(4,1)}, u32[]{:S(2)}) copy-start(pred[4,128,512]{2,1,0:T(8,128)(4,1)} %broadcast_and_fusion) | copy-start | bytes 786436
  1476.3 45.5 %copy-start.5 = (f32[128,1,128]{0,2,1:T(8,128)S(1)}, f32[128,1,128]{0,2,1:T(8,128)}, u32[]{:S(2)}) copy-start(f32[128,1,128]{0,2,1:T(8,128)} %copy-done.4) | copy-start | bytes 196612
  1476.3 45.5 %copy-start.8 = (f32[128,1,128]{0,2,1:T(8,128)S(1)}, f32[128,1,128]{0,2,1:T(8,128)}, u32[]{:S(2)}) copy-start(f32[128,1,128]{0,2,1:T(8,128)} %fusion.113) | copy-start | bytes 196612
  1521.8 23.1 %copy-start.10 = (f32[4,128]{1,0:T(4,128)S(1)}, f32[4,128]{1,0:T(4,128)}, u32[]{:S(2)}) copy-start(f32[4,128]{1,0:T(4,128)} %copy-done.9) | copy-start | bytes 6148
  1521.8 23.1 %copy-start.12 = (f32[4,128]{1,0:T(4,128)S(1)}, f32[4,128]{1,0:T(4,128)}, u32[]{:S(2)}) copy-start(f32[4,128]{1,0:T(4,128)} %copy-done.11) | copy-start | bytes 6148
  1555.8 6.9 copy-start.13
  1555.8 7.0 copy-start.14
  1562.8 44.0 %copy-start.1 = (f32[1,512,1,8,64]{1,4,0,3,2:T(8,128)S(1)}, f32[1,512,1,8,64]{1,4,0,3,2:T(8,128)}, u32[]{:S(2)}) copy-start(f32[1,512,1,8,64]{1,4,0,3,2:T(8,128)} %get-tuple-element.11) | copy-start | bytes 3145732
  1562.8 44.0 %copy-start.2 = (f32[1,512,1,8,64]{1,4,0,3,2:T(8,128)S(1)}, f32[1,512,1,8,64]{1,4,0,3,2:T(8,128)}, u32[]{:S(2)}) copy-start(f32[1,512,1,8,64]{1,4,0,3,2:T(8,128)} %get-tuple-element.12) | copy-start | bytes 3145732
  1562.8 44.0 %copy-start.3 = (f32[1,512,1,8,64]{1,4,0,3,2:T(8,128)S(1)}, f32[1,512,1,8,64]{1,4,0,3,2:T(8,128)}, u32[]{:S(2)}) copy-start(f32[1,512,1,8,64]{1,4,0,3,2:T(8,128)} %get-tuple-element.13) | copy-start | bytes 3145732
  1718.7 368.4 %all-to-all-start.1 = ((f32[1,32,16,8192]{3,2,0,1:T(8,128)}), f32[1,32,16,8192]{3,2,0,1:T(8,128)}, u32[]{:S(2)}, u32[]{:S(2)}) async-start(f32[1,32,16,8192]{3,2,0,1:T(8,128)} %bitcast.171), calls=%async_computation.1 | async-start | bytes 33554432 | tf_op jit(solution)/shard_map/all_to_all | solution.py:119
where the time goes:
time: 2130 us; the launch traced here: 2120 us
  waiting for transfers between devices  1070 us (50%)
  matrix products  775 us (36%)
  local copies, waits for them, and re-layouts  157 us (7%)
  other arithmetic  110 us (5%)
    all_to_all x1, waiting for transfers between devices, on_device(): lax.all_to_all(sent, ('gx', 'gy'), split_axis=1, concat_axis=1, tiled=True)  705 us
    dot_general x1, matrix products, on_device(): jnp.einsum('fdspkjy,psyrq->fdrkjq', moved, y_forward, precision=exact_mode)  433 us
    all_to_all x1, waiting for transfers between devices, on_device(): lax.all_to_all(sent_back, ('gx', 'gy'), split_axis=1, concat_axis=1, tile...  360 us
    dot_general x1, matrix products, on_device(): jnp.einsum('fdpkjq,pdra->farkjq', planes, block_forward, precision=exact_...  74.9 us
    dot_general x2, matrix products, depth_forward(): lax.dot_general(forward_depth, flat_lines, (((1,), (1,)), ((), ())), prec...  62.1 us
    dot_general x1, matrix products, on_device(): jnp.einsum('fdpkjq,pqrsy->fdsrkjy', blocks, y_inverse, precision=exact_mode)  60.9 us
    reshape x1, local copies, waits for them, and re-layouts, on_device(): moved = moved.reshape(2, count_x, count_y, 2, kz_slices, x_local, y_local)  52.6 us
    dot_general x1, matrix products, on_device(): jnp.einsum('fapkjq,pjrb->farkbq', turned, local_forward, precision=exact_...  45.4 us
  transfers between devices with their start and end apart: 2, of which 2 were waited for; matrix products, arithmetic and copies ran while one was open for 1% of the time, Pallas kernels for 0%

commit v1 on v0

v1 whole, which is shorter than its diff:
```python
import math

import jax
import jax.numpy as jnp
import numpy as np
from jax import lax
from jax.sharding import PartitionSpec as P

split_mode = lax.Precision.HIGH


def phases(numerator, denominator):
    radians = (numerator % denominator) * (2.0 * math.pi / denominator)
    return np.cos(radians), np.sin(radians)


def base_table(length):
    positions = np.arange(length)
    cosines, sines = phases(positions[:, None] * positions[None, :], length)
    return cosines.astype(np.float32), sines.astype(np.float32)


def complex_table(base, direction):
    cosines, sines = base
    signed = direction * sines
    real_rows = jnp.stack([cosines, signed], axis=1)
    imag_rows = jnp.stack([-signed, cosines], axis=1)
    return jnp.stack([real_rows, imag_rows], axis=0)


def depth_tables(depth_cells, devices, kz_slices, chunk, chunk_slices, scale):
    wave = (
        np.arange(devices)[:, None] * kz_slices
        + chunk * chunk_slices
        + np.arange(chunk_slices)[None, :]
    )
    cosines, sines = phases(wave[:, :, None] * np.arange(depth_cells), depth_cells)
    weight = np.where(wave == 0, 1.0, 2.0)[:, :, None] * scale
    forward = np.stack([cosines, -sines], axis=1).reshape(-1, depth_cells)
    inverse = np.stack([weight * cosines, -weight * sines], axis=1).reshape(-1, depth_cells)
    return forward.astype(np.float32), inverse.astype(np.float32)


def on_device(density_one, density_two):
    count_x = lax.axis_size("gx")
    count_y = lax.axis_size("gy")
    devices = count_x * count_y
    x_local, y_local, depth_cells = density_one.shape
    grid_x = x_local * count_x
    grid_y = y_local * count_y
    kz_slices = depth_cells // 2 // devices
    cell_total = float(grid_x * grid_y * depth_cells)
    chunks = 2 if kz_slices % 2 == 0 else 1
    per_chunk = kz_slices // chunks

    base_x = base_table(grid_x)
    base_y = base_x if grid_y == grid_x else base_table(grid_y)
    x_forward = complex_table(base_x, -1.0).reshape(2, count_x, x_local, 2, grid_x)
    x_inverse = complex_table(base_x, 1.0).reshape(2, grid_x, 2, count_x, x_local)
    y_forward = complex_table(base_y, -1.0).reshape(2, count_y, y_local, 2, grid_y)
    y_inverse = jnp.stack(base_y, axis=1).reshape(grid_y, 2, count_y, y_local)
    tables = [
        depth_tables(depth_cells, devices, kz_slices, chunk, per_chunk, 1.0 / math.sqrt(cell_total))
        for chunk in range(chunks)
    ]
    keep_x = np.arange(grid_x) != grid_x // 2
    keep_y = np.arange(grid_y) != grid_y // 2
    keep = keep_y[:, None, None] & keep_x[None, None, :]

    def exchange(rows):
        return lax.all_to_all(rows, ("gx", "gy"), split_axis=0, concat_axis=0, tiled=True)

    def product(pattern, left, right):
        return jnp.einsum(pattern, left, right, precision=split_mode)

    def depth_forward(density, table):
        lines = product("gz,xyz->gyx", table, density)
        return exchange(lines.reshape(devices, 2 * per_chunk, y_local * x_local))

    def plane_forward(rows):
        rows = rows.reshape(count_x, count_y, 2, per_chunk, y_local, x_local)
        lines = product("dspkyx,pdxrw->skyrw", rows, x_forward)
        return product("skyrw,rsytq->tqkw", lines, y_forward)

    moved = [
        [depth_forward(density, forward) for density in (density_one, density_two)]
        for forward, _ in tables
    ]
    correlation = None
    for (one, two), (_, inverse) in zip(moved, tables):
        first = plane_forward(one)
        second = plane_forward(two)
        power = (first[0] * second[0] + first[1] * second[1]) / cell_total
        power = jnp.where(keep, power, 0.0)
        lines = product("qkw,qrsy->srkyw", power, y_inverse)
        blocks = product("srkyw,rwpdx->dspkyx", lines, x_inverse)
        back = exchange(blocks.reshape(devices, 2 * per_chunk, y_local * x_local))
        back = back.reshape(devices * 2 * per_chunk, y_local, x_local)
        part = product("gyx,gz->xyz", back, inverse)
        correlation = part if correlation is None else correlation + part
    return correlation


def solution(mesh):
    return jax.shard_map(
        on_device,
        mesh=mesh,
        in_specs=(P("gx", "gy", None), P("gx", "gy", None)),
        out_specs=P("gx", "gy", None),
        check_vma=False,
    )
```

time: 2130 us -> 1250 us (0.59)
  matrix products: 775 us -> 309 us
  waiting for transfers between devices: 1070 us -> 750 us
  other arithmetic: 110 us -> 0.01 us
    dot_general x9 -> x18, matrix products: 775 us -> 309 us  [product(): return jnp.einsum(pattern, left, right, precision=split_mode)]
    all_to_all x2 -> x6, waiting for transfers between devices: 1070 us -> 750 us  [exchange(): lax.all_to_all(rows, ('gx', 'gy'), split_axis=0, concat_axis=0, tiled=True)]
    another operation x5 -> x0, other arithmetic: 43.1 us -> none  [the longest x1 23 us: on_device(): jnp.stack([real_part * forward_cos + imag_part * forward_sin, imag_part *...]
    unnamed x38 -> x33, local copies, waits for them, and re-layouts: 1.1 us -> 33.8 us
    add x3 -> x0, other arithmetic: 27.3 us -> none  [the longest x1 27.3 us: on_device(): real_part * forward_cos + imag_part * forward_sin]
    reshape x2 -> x6, local copies, waits for them, and re-layouts: 80.5 us -> 56.7 us  [the longest x4 37.7 us: depth_forward(): return exchange(lines.reshape(devices, 2 * per_chunk, y_local * x_local))]
    transpose x2 -> x6, local copies, waits for them, and re-layouts: 62.3 us -> 41.5 us  [product(): return jnp.einsum(pattern, left, right, precision=split_mode)]
  transfers between devices with their start and end apart: 2 -> 6, of which waited for: 2 -> 6; matrix products, arithmetic and copies ran while one was open for 1% -> 29% of each run, Pallas kernels for 0% -> 0%
where the time goes in v1:
time: 1250 us; the launch traced here: 1240 us
  waiting for transfers between devices  750 us (60%)
  matrix products  309 us (25%)
  local copies, waits for them, and re-layouts  150 us (12%)
  starting transfers between devices  27.5 us (2%)
    all_to_all x6, waiting for transfers between devices, exchange(): lax.all_to_all(rows, ('gx', 'gy'), split_axis=0, concat_axis=0, tiled=True)  750 us
    dot_general x18, matrix products, product(): return jnp.einsum(pattern, left, right, precision=split_mode)  309 us
    transpose x6, local copies, waits for them, and re-layouts, product(): return jnp.einsum(pattern, left, right, precision=split_mode)  41.5 us
    reshape x4, local copies, waits for them, and re-layouts, depth_forward(): return exchange(lines.reshape(devices, 2 * per_chunk, y_local * x_local))  37.7 us
    unnamed x33, local copies, waits for them, and re-layouts  33.8 us
    all_to_all x6, starting transfers between devices, exchange(): lax.all_to_all(rows, ('gx', 'gy'), split_axis=0, concat_axis=0, tiled=True)  27.5 us
  transfers between devices with their start and end apart: 6, of which 6 were waited for; matrix products, arithmetic and copies ran while one was open for 29% of the time, Pallas kernels for 0%

profile of v1, /device:TPU:0, one launch (start us, length us, event | category | flops | bytes accessed | tf_op | source)
XLA Modules:
  0.0 1237.3 jit_solution(255929885970680652)
XLA Ops:
  0.0 21.4 %fusion.56 = f32[256,64,128]{2,0,1:T(8,128)S(1)} fusion(f32[256,512,1]{1,0,2:T(8,128)} %constant.58, f32[128,64,512]{2,1,0:T(8,128)} %param.23), kind=kOutput, calls=%fused_computation.57 | convolution fusion | flops 6442450944 | bytes 25690112 | tf_op jit(solution)/shard_map/gz,xyz->gyx/dot_general | solution.py:74
  21.4 8.3 copy.93
  29.7 9.5 reshape.96
  39.1 7.6 all-to-all-start.3
  46.8 0.0 copy-done.1
  46.8 21.3 %fusion.53 = f32[256,64,128]{2,0,1:T(8,128)S(1)} fusion(f32[256,512,1]{1,0,2:T(8,128)S(1)} %copy-done.1, f32[128,64,512]{2,1,0:T(8,128)} %param.23), kind=kOutput, calls=%fused_computation.56 | convolution fusion | flops 6442450944 | bytes 25690112 | tf_op jit(solution)/shard_map/gz,xyz->gyx/dot_general | solution.py:74
  68.1 8.3 copy.85
  76.4 9.5 reshape.90
  85.8 145.7 %all-to-all-done.3 = f32[32,8,8192]{2,1,0:T(8,128)} async-done(((f32[32,8,8192]{2,1,0:T(8,128)}), f32[32,8,8192]{2,1,0:T(8,128)}, u32[]{:S(2)}, u32[]{:S(2)}) %all-to-all-start.3) | async-done | bytes 8388640 | tf_op jit(solution)/shard_map/all_to_all | solution.py:71
  231.5 3.9 all-to-all-start
  235.4 0.0 copy-done.2
  235.4 21.3 %fusion.62 = f32[256,64,128]{2,0,1:T(8,128)S(1)} fusion(f32[256,512,1]{1,0,2:T(8,128)S(1)} %copy-done.2, f32[128,64,512]{2,1,0:T(8,128)} %param.24), kind=kOutput, calls=%fused_computation.59 | convolution fusion | flops 6442450944 | bytes 25690112 | tf_op jit(solution)/shard_map/gz,xyz->gyx/dot_general | solution.py:74
  256.8 8.3 copy.96
  265.0 9.4 reshape.98
  274.4 145.8 %all-to-all-done = f32[32,8,8192]{2,1,0:T(8,128)} async-done(((f32[32,8,8192]{2,1,0:T(8,128)}), f32[32,8,8192]{2,1,0:T(8,128)}, u32[]{:S(2)}, u32[]{:S(2)}) %all-to-all-start) | async-done | bytes 8388640 | tf_op jit(solution)/shard_map/all_to_all | solution.py:71
  420.2 4.1 all-to-all-start.4
  424.3 21.3 %fusion.59 = f32[256,64,128]{2,0,1:T(8,128)S(1)} fusion(f32[256,512,1]{1,0,2:T(8,128)S(1)} %copy-done.1, f32[128,64,512]{2,1,0:T(8,128)} %param.24), kind=kOutput, calls=%fused_computation.58 | convolution fusion | flops 6442450944 | bytes 25690112 | tf_op jit(solution)/shard_map/gz,xyz->gyx/dot_general | solution.py:74
  445.6 8.3 copy.88
  453.9 9.4 reshape.92
  463.3 145.7 %all-to-all-done.4 = f32[32,8,8192]{2,1,0:T(8,128)} async-done(((f32[32,8,8192]{2,1,0:T(8,128)}), f32[32,8,8192]{2,1,0:T(8,128)}, u32[]{:S(2)}, u32[]{:S(2)}) %all-to-all-start.4) | async-done | bytes 8388640 | tf_op jit(solution)/shard_map/all_to_all | solution.py:71
  609.1 3.9 all-to-all-start.1
  612.9 0.0 copy-done.5
  612.9 0.1 copy.189
  613.1 5.0 copy.134
  618.1 0.0 copy-start.8
  618.1 5.2 copy.135
  623.3 0.0 copy-done.8
  623.3 13.9 %fusion.22 = f32[8,4,64,2,512,1,1]{4,2,6,1,0,3,5:T(8,128)S(1)} fusion(f32[2,4,128,2,512,1,1]{4,2,0,6,5,3,1:T(8,128)S(1)} %copy-done.8, f32[4,8,2,4,64,128,1]{5,4,3,2,1,0,6:T(8,128)S(1)} %bitcast.179), kind=kOutput, calls=%fused_computation.23 | convolution fusion | flops 12884901888 | bytes 20971520 | tf_op jit(solution)/shard_map/dspkyx,pdxrw->skyrw/dot_general | solution.py:74
  637.2 0.0 copy-start.6
  637.2 14.1 %fusion.20 = f32[8,4,64,2,512,1,1]{4,2,6,1,0,3,5:T(8,128)S(1)} fusion(f32[2,4,128,2,512,1,1]{4,2,0,6,5,3,1:T(8,128)S(1)} %copy-done.8, f32[4,8,2,4,64,128,1]{5,4,3,2,1,0,6:T(8,128)S(1)} %bitcast.180), kind=kOutput, calls=%fused_computation.21 | convolution fusion | flops 12884901888 | bytes 20971520 | tf_op jit(solution)/shard_map/dspkyx,pdxrw->skyrw/dot_general | solution.py:74
  651.3 0.0 copy-done.6
  651.3 15.3 %fusion.74 = f32[2,512,4,512]{3,1,2,0:T(8,128)S(1)} fusion(f32[2,8,64,2,512,1]{4,2,1,0,5,3:T(8,128)S(1)} %copy-done.6, f32[8,4,64,2,512,1,1]{4,2,6,1,0,3,5:T(8,128)S(1)} %fusion.22), kind=kOutput, calls=%fused_computation.63 | convolution fusion | flops 12884901888 | bytes 20971520 | tf_op jit(solution)/shard_map/skyrw,rsytq->tqkw/dot_general | solution.py:74
  666.5 0.0 copy-start
  666.6 16.2 %fusion.77 = f32[2,512,4,512]{3,1,2,0:T(8,128)} fusion(f32[2,8,64,2,512,1]{4,2,1,0,5,3:T(8,128)S(1)} %copy-done.6, f32[8,4,64,2,512,1,1]{4,2,6,1,0,3,5:T(8,128)S(1)} %fusion.20), kind=kOutput, calls=%fused_computation.64 | convolution fusion | flops 12884901888 | bytes 20971520 | tf_op jit(solution)/shard_map/skyrw,rsytq->tqkw/dot_general | solution.py:74
  682.7 0.0 copy-done
  682.7 10.9 fusion.40
  693.6 16.5 %fusion.80 = f32[4,8,2,4,64,128]{5,4,3,1,0,2:T(8,128)S(1)} fusion(f32[2,512,2,4,128,1,1]{4,1,0,6,5,3,2:T(8,128)} %constant.52, f32[2,8,64,4,512]{4,2,0,3,1:T(8,128)S(1)} %fusion.40), kind=kOutput, calls=%fused_computation.65 | convolution fusion | flops 12884901888 | bytes 20971520 | tf_op jit(solution)/shard_map/srkyw,rwpdx->dspkyx/dot_general | solution.py:74
  710.1 4.2 copy.98
  714.4 9.5 reshape.100
  723.8 73.7 %all-to-all-done.1 = f32[32,8,8192]{2,1,0:T(8,128)} async-done(((f32[32,8,8192]{2,1,0:T(8,128)}), f32[32,8,8192]{2,1,0:T(8,128)}, u32[]{:S(2)}, u32[]{:S(2)}) %all-to-all-start.1) | async-done | bytes 8388640 | tf_op jit(solution)/shard_map/all_to_all | solution.py:71
  797.6 4.2 all-to-all-start.5
  801.7 5.0 copy.131
  806.7 5.0 copy.132
  811.8 0.0 copy-start.9
  811.8 17.0 %fusion.26 = f32[8,4,64,2,512,1,1]{4,2,6,1,0,3,5:T(8,128)} fusion(f32[2,4,128,2,512,1,1]{4,2,0,6,5,3,1:T(8,128)} %constant.56, f32[4,8,2,4,64,128,1]{5,4,3,2,1,0,6:T(8,128)S(1)} %bitcast.181), kind=kOutput, calls=%fused_computation.27 | convolution fusion | flops 12884901888 | bytes 20971520 | tf_op jit(solution)/shard_map/dspkyx,pdxrw->skyrw/dot_general | solution.py:74
  828.8 0.0 copy-done.9
  828.8 15.7 %fusion.24 = f32[8,4,64,2,512,1,1]{4,2,6,1,0,3,5:T(8,128)} fusion(f32[2,4,128,2,512,1,1]{4,2,0,6,5,3,1:T(8,128)S(1)} %copy-done.9, f32[4,8,2,4,64,128,1]{5,4,3,2,1,0,6:T(8,128)S(1)} %bitcast.178), kind=kOutput, calls=%fused_computation.25 | convolution fusion | flops 12884901888 | bytes 20971520 | tf_op jit(solution)/shard_map/dspkyx,pdxrw->skyrw/dot_general | solution.py:74
  844.5 21.6 %fusion.65 = f32[2,512,4,512]{3,1,2,0:T(8,128)S(1)} fusion(f32[2,8,64,2,512,1]{4,2,1,0,5,3:T(8,128)S(1)} %copy-done.7, f32[8,4,64,2,512,1,1]{4,2,6,1,0,3,5:T(8,128)} %fusion.26), kind=kOutput, calls=%fused_computation.60 | convolution fusion | flops 12884901888 | bytes 20971520 | tf_op jit(solution)/shard_map/skyrw,rsytq->tqkw/dot_general | solution.py:74
  866.1 16.2 %fusion.68 = f32[2,512,4,512]{3,1,2,0:T(8,128)} fusion(f32[2,8,64,2,512,1]{4,2,1,0,5,3:T(8,128)S(1)} %copy-done.7, f32[8,4,64,2,512,1,1]{4,2,6,1,0,3,5:T(8,128)S(1)} %copy-done.10), kind=kOutput, calls=%fused_computation.61 | convolution fusion | flops 12884901888 | bytes 20971520 | tf_op jit(solution)/shard_map/skyrw,rsytq->tqkw/dot_general | solution.py:74
  882.3 10.9 fusion.49
  893.2 16.7 %fusion.71 = f32[4,8,2,4,64,128]{5,4,3,1,0,2:T(8,128)S(1)} fusion(f32[2,512,2,4,128,1,1]{4,1,0,6,5,3,2:T(8,128)} %constant.52, f32[2,8,64,4,512]{4,2,0,3,1:T(8,128)S(1)} %fusion.49), kind=kOutput, calls=%fused_computation.62 | convolution fusion | flops 12884901888 | bytes 20971520 | tf_op jit(solution)/shard_map/srkyw,rwpdx->dspkyx/dot_general | solution.py:74
  909.9 4.2 copy.90
  914.1 9.5 reshape.94
  923.6 62.9 %all-to-all-done.5 = f32[32,8,8192]{2,1,0:T(8,128)} async-done(((f32[32,8,8192]{2,1,0:T(8,128)}), f32[32,8,8192]{2,1,0:T(8,128)}, u32[]{:S(2)}, u32[]{:S(2)}) %all-to-all-start.5) | async-done | bytes 8388640 | tf_op jit(solution)/shard_map/all_to_all | solution.py:71
  986.5 3.9 all-to-all-start.2
  990.4 8.3 copy.136
  998.6 176.5 %all-to-all-done.2 = f32[32,8,8192]{2,1,0:T(8,128)} async-done(((f32[32,8,8192]{2,1,0:T(8,128)}), f32[32,8,8192]{2,1,0:T(8,128)}, u32[]{:S(2)}, u32[]{:S(2)}) %all-to-all-start.2) | async-done | bytes 8388640 | tf_op jit(solution)/shard_map/all_to_all | solution.py:71
  1175.1 5.2 copy.133
  1180.3 0.0 slice-start.1
  1180.3 0.0 copy-start.4
  1180.3 17.5 %fusion.33 = f32[64,128,512]{2,1,0:T(8,128)} fusion(f32[256,512,1]{1,0,2:T(8,128)S(1)} %copy-done.3, f32[256,64,128]{2,1,0:T(8,128)S(1)} %bitcast.174), kind=kOutput, calls=%fused_computation.34 | convolution fusion | flops 6442450944 | bytes 25690112 | tf_op jit(solution)/shard_map/gyx,gz->xyz/dot_general | solution.py:74
  1197.9 0.0 slice-done.1
  1197.9 21.4 %add_bitcast_fusion = f32[128,64,512]{2,0,1:T(8,128)} fusion(f32[64,128,512]{2,1,0:T(8,128)} %fusion.33, f32[256,512,1]{1,0,2:T(8,128)S(1)} %copy-done.4, f32[256,64,128]{2,1,0:T(8,128)S(1)} %bitcast.177), kind=kOutput, calls=%fused_computation | convolution fusion | flops 6446645248 | bytes 42467328 | tf_op jit(solution)/shard_map/gyx,gz->xyz/dot_general | solution.py:74
  1219.3 17.8 %copy.100 = f32[128,64,512]{2,1,0:T(8,128)} copy(f32[128,64,512]{2,0,1:T(8,128)} %add_bitcast_fusion) | data formatting | bytes 33554432 | tf_op jit(solution)/shard_map/add | solution.py:100
  (13 shorter events, 0.0 us)
Async XLA Ops:
  39.1 7.6 copy-start.1
  39.1 192.4 %all-to-all-start.3 = ((f32[32,8,8192]{2,1,0:T(8,128)}), f32[32,8,8192]{2,1,0:T(8,128)}, u32[]{:S(2)}, u32[]{:S(2)}) async-start(f32[32,8,8192]{2,1,0:T(8,128)} %reshape.96), calls=%async_computation.3 | async-start | bytes 16777216 | tf_op jit(solution)/shard_map/all_to_all | solution.py:71
  85.8 149.6 %copy-start.2 = (f32[256,512,1]{1,0,2:T(8,128)S(1)}, f32[256,512,1]{1,0,2:T(8,128)}, u32[]{:S(2)}) copy-start(f32[256,512,1]{1,0,2:T(8,128)} %constant.58) | copy-start | bytes 1572868
  231.5 188.7 %all-to-all-start = ((f32[32,8,8192]{2,1,0:T(8,128)}), f32[32,8,8192]{2,1,0:T(8,128)}, u32[]{:S(2)}, u32[]{:S(2)}) async-start(f32[32,8,8192]{2,1,0:T(8,128)} %reshape.90), calls=%async_computation | async-start | bytes 16777216 | tf_op jit(solution)/shard_map/all_to_all | solution.py:71
  420.2 188.9 %all-to-all-start.4 = ((f32[32,8,8192]{2,1,0:T(8,128)}), f32[32,8,8192]{2,1,0:T(8,128)}, u32[]{:S(2)}, u32[]{:S(2)}) async-start(f32[32,8,8192]{2,1,0:T(8,128)} %reshape.98), calls=%async_computation.4 | async-start | bytes 16777216 | tf_op jit(solution)/shard_map/all_to_all | solution.py:71
  463.3 149.6 %copy-start.5 = (pred[512,512]{1,0:T(32,128)(4,1)S(1)}, pred[512,512]{1,0:T(32,128)(4,1)}, u32[]{:S(2)}) copy-start(pred[512,512]{1,0:T(32,128)(4,1)} %constant.39) | copy-start | bytes 786436
  609.1 188.5 %all-to-all-start.1 = ((f32[32,8,8192]{2,1,0:T(8,128)}), f32[32,8,8192]{2,1,0:T(8,128)}, u32[]{:S(2)}, u32[]{:S(2)}) async-start(f32[32,8,8192]{2,1,0:T(8,128)} %reshape.92), calls=%async_computation.1 | async-start | bytes 16777216 | tf_op jit(solution)/shard_map/all_to_all | solution.py:71
  618.1 5.2 copy-start.8
  637.2 14.1 %copy-start.6 = (f32[2,8,64,2,512,1]{4,2,1,0,5,3:T(8,128)S(1)}, f32[2,8,64,2,512,1]{4,2,1,0,5,3:T(8,128)}, u32[]{:S(2)}) copy-start(f32[2,8,64,2,512,1]{4,2,1,0,5,3:T(8,128)} %constant.54) | copy-start | bytes 12582916
  666.5 16.2 %copy-start = (f32[512,2,8,64,1]{0,3,1,4,2:T(8,128)S(1)}, f32[512,2,8,64,1]{0,3,1,4,2:T(8,128)}, u32[]{:S(2)}) copy-start(f32[512,2,8,64,1]{0,3,1,4,2:T(8,128)} %constant.53) | copy-start | bytes 6291460
  797.6 188.9 %all-to-all-start.5 = ((f32[32,8,8192]{2,1,0:T(8,128)}), f32[32,8,8192]{2,1,0:T(8,128)}, u32[]{:S(2)}, u32[]{:S(2)}) async-start(f32[32,8,8192]{2,1,0:T(8,128)} %reshape.100), calls=%async_computation.5 | async-start | bytes 16777216 | tf_op jit(solution)/shard_map/all_to_all | solution.py:71
  811.8 17.0 %copy-start.9 = (f32[2,4,128,2,512,1,1]{4,2,0,6,5,3,1:T(8,128)S(1)}, f32[2,4,128,2,512,1,1]{4,2,0,6,5,3,1:T(8,128)}, u32[]{:S(2)}) copy-start(f32[2,4,128,2,512,1,1]{4,2,0,6,5,3,1:T(8,128)} %constant.56) | copy-start | bytes 12582916
  828.8 15.7 %copy-start.7 = (f32[2,8,64,2,512,1]{4,2,1,0,5,3:T(8,128)S(1)}, f32[2,8,64,2,512,1]{4,2,1,0,5,3:T(8,128)}, u32[]{:S(2)}) copy-start(f32[2,8,64,2,512,1]{4,2,1,0,5,3:T(8,128)} %constant.54) | copy-start | bytes 12582916
  844.5 21.6 %copy-start.10 = (f32[8,4,64,2,512,1,1]{4,2,6,1,0,3,5:T(8,128)S(1)}, f32[8,4,64,2,512,1,1]{4,2,6,1,0,3,5:T(8,128)}, u32[]{:S(2)}) copy-start(f32[8,4,64,2,512,1,1]{4,2,6,1,0,3,5:T(8,128)} %fusion.24) | copy-start | bytes 25165828
  986.5 188.6 %all-to-all-start.2 = ((f32[32,8,8192]{2,1,0:T(8,128)}), f32[32,8,8192]{2,1,0:T(8,128)}, u32[]{:S(2)}, u32[]{:S(2)}) async-start(f32[32,8,8192]{2,1,0:T(8,128)} %reshape.94), calls=%async_computation.2 | async-start | bytes 16777216 | tf_op jit(solution)/shard_map/all_to_all | solution.py:71
  1175.1 5.2 copy-start.3
  1175.1 22.8 %slice-start = ((s8[8388608]{0:T(1024)(128)(4,1)}), s8[4194304]{0:T(1024)(128)(4,1)S(1)}, s32[]{:S(2)}) async-start(s8[8388608]{0:T(1024)(128)(4,1)} %bitcast.175), calls=%async_computation.6 | async-start | bytes 8388608
  1180.3 17.6 %slice-start.1 = ((s8[8388608]{0:T(1024)(128)(4,1)}), s8[4194304]{0:T(1024)(128)(4,1)S(1)}, s32[]{:S(2)}) async-start(s8[8388608]{0:T(1024)(128)(4,1)} %bitcast.175), calls=%async_computation.7 | async-start | bytes 8388608
  1180.3 17.6 %copy-start.4 = (f32[256,512,1]{1,0,2:T(8,128)S(1)}, f32[256,512,1]{1,0,2:T(8,128)}, u32[]{:S(2)}) copy-start(f32[256,512,1]{1,0,2:T(8,128)} %constant.59) | copy-start | bytes 1572868
